TPU v7x, 128 devices: a whole 4x4x4 slice. The times are simulated.
128 devices in a mesh: gx: 16 (over z, y), gy: 8 (over x, core).
Axes of the slice: x: 4, y: 4, z: 4, core: 2. Of those that a mesh axis runs over, the one named last changes fastest.
Arguments:
- pumping: float32 [16, 4, 128, 1024], P(None, None, 'gx', 'gy'), may hold values from -1080 to 1080
- conductivity: float32 [4, 128, 1024], P(None, 'gx', 'gy'), may hold values from 0.2 to 5
- capacity: float32 [4, 128, 1024], P(None, 'gx', 'gy'), may hold values from 1 to 10
Outputs:
- solution: float32 [16, 4, 128, 1024], P(None, None, 'gx', 'gy')
- residual: float32 [16, 4, 128, 1024], P(None, None, 'gx', 'gy')
All inputs are finite; a program needn't handle non-finite values.
Results may differ from a plain program's by a relative error of at most 0.0035.
Values sent between devices are 32-bit elements; how exact they have to be, the bound alone decides.
A program may use at most 64 MiB of HBM per device.

v0:
```python
import jax
import jax.numpy as jnp
from jax import lax
from jax.sharding import PartitionSpec as P

RHS = 16
S = 4
CYCLES = 5
BASIS = 80


def padded_2(array, sides, width):
    for axis, dim in sides:
        devices, length = (lax.axis_size(axis), array.shape[dim])
        up = [(i, (i + 1) % devices) for i in range(devices - 1)]
        down = [(j, i) for i, j in up]
        last = lax.slice_in_dim(array, length - width, length, axis=dim)
        leading = lax.slice_in_dim(array, 0, width, axis=dim)
        before = lax.ppermute(last, axis, up)
        after = lax.ppermute(leading, axis, down)
        array = jnp.concatenate([before, array, after], axis=dim)
    return array


def face_terms(padded, storage):
    core = padded[1:-1, 1:-1, 1:-1]
    terms = (
        (core + padded[:-2, 1:-1, 1:-1]) * 0.5,
        (core + padded[2:, 1:-1, 1:-1]) * 0.5,
        (core + padded[1:-1, :-2, 1:-1]) * 0.5,
        (core + padded[1:-1, 2:, 1:-1]) * 0.5,
        (core + padded[1:-1, 1:-1, :-2]) * 0.5,
        (core + padded[1:-1, 1:-1, 2:]) * 0.5,
    )
    diagonal = storage + terms[0] + terms[1] + terms[2] + terms[3] + terms[4] + terms[5]
    return (terms, diagonal)


def apply_off(padded, terms):
    total = terms[0] * padded[:, :-2, 1:-1, 1:-1] + terms[1] * padded[:, 2:, 1:-1, 1:-1]
    total = total + terms[2] * padded[:, 1:-1, :-2, 1:-1] + terms[3] * padded[:, 1:-1, 2:, 1:-1]
    total = total + terms[4] * padded[:, 1:-1, 1:-1, :-2] + terms[5] * padded[:, 1:-1, 1:-1, 2:]
    return total


def small_solve(gram_all):
    shift_matrix = jnp.eye(BASIS, BASIS - RHS, dtype=jnp.float32) + jnp.eye(
        BASIS, BASIS - RHS, k=-RHS, dtype=jnp.float32
    )
    first_block = jnp.eye(BASIS, RHS, dtype=jnp.float32)
    hp = lax.Precision.HIGHEST
    gram_shift = jnp.dot(gram_all, shift_matrix, precision=hp)
    normal = jnp.dot(shift_matrix.T, gram_shift, precision=hp)
    right_side = jnp.dot(gram_shift.T, first_block, precision=hp)
    lower = jnp.linalg.cholesky(normal)
    y = jax.scipy.linalg.cho_solve((lower, True), right_side)
    coeffs = first_block - jnp.dot(shift_matrix, y, precision=hp)
    return (y, coeffs)


def shards(pumping, conductivity, capacity):
    hp = lax.Precision.HIGHEST
    shape = pumping.shape
    cond_halo = padded_2(conductivity, (("gx", 1), ("gy", 2)), 1)
    cond_pad = jnp.pad(cond_halo, ((1, 1), (0, 0), (0, 0)))
    terms, diagonal = face_terms(cond_pad, capacity)
    solution = jnp.zeros(shape, jnp.float32)
    residual = pumping / diagonal
    for restart in range(CYCLES):
        blocks = [residual]
        for k in range(S):
            bordered = padded_2(blocks[-1], (("gx", 2), ("gy", 3)), 1)
            padded = jnp.pad(bordered, ((0, 0), (1, 1), (0, 0), (0, 0)))
            blocks.append(-apply_off(padded, terms) / diagonal)
        stacked = jnp.concatenate(blocks, 0).reshape(BASIS, -1)
        local_gram = jnp.dot(stacked, stacked.T, precision=hp)
        gram_all = lax.psum(local_gram, ("gx", "gy"))
        y, coeffs = small_solve(gram_all)
        solution = solution + jnp.dot(y.T, stacked[: BASIS - RHS], precision=hp).reshape(shape)
        residual = jnp.dot(coeffs.T, stacked, precision=hp).reshape(shape)
    return (solution, residual)


def solution(mesh):
    return jax.shard_map(
        shards,
        mesh=mesh,
        in_specs=(P(None, None, "gx", "gy"), P(None, "gx", "gy"), P(None, "gx", "gy")),
        out_specs=(P(None, None, "gx", "gy"), P(None, None, "gx", "gy")),
        check_vma=False,
    )
```

profile of v0, /device:TPU:1, one launch (start us, length us, event | category | flops | bytes accessed | tf_op | source)
XLA Modules:
  0.0 885.2 jit_solution(18000092713170605420)
XLA Ops:
  10.6 5.1 collective-permute-start.2
  39.3 4.4 collective-permute-done.7
  44.5 4.6 collective-permute-start.8
  82.1 4.4 collective-permute-done.15
  103.1 4.4 collective-permute-done.19
  109.9 68.0 %psum.35 = f32[80,80]{1,0:T(8,128)S(1)} all-reduce(f32[80,80]{1,0:T(8,128)S(1)} %convolution_bitcast_fusion.4), channel_id=1, replica_groups=mesh['gx'=16,'gy'=8] {'gx','gy'}, use_global_device_ids=true, to_apply=%region_0.1 | all-reduce | flops 6400 | bytes 51200 | tf_op jit(solution)/shard_map/psum | solution.py:77
  179.8 5.8 cholesky.89
  187.0 4.9 custom-call.11
  201.0 4.9 collective-permute-start.22
  235.3 4.8 collective-permute-start.28
  280.8 66.5 %psum.36 = f32[80,80]{1,0:T(8,128)} all-reduce(f32[80,80]{1,0:T(8,128)} %convolution_bitcast_fusion.3), channel_id=1, replica_groups=mesh['gx'=16,'gy'=8] {'gx','gy'}, use_global_device_ids=true, to_apply=%region_3.6 | all-reduce | flops 6400 | bytes 51200 | tf_op jit(solution)/shard_map/psum | solution.py:77
  352.3 5.8 cholesky.100
  359.5 4.9 custom-call.12
  408.2 5.4 collective-permute-start.44
  425.6 4.4 collective-permute-done.47
  454.5 66.5 %psum.37 = f32[80,80]{1,0:T(8,128)S(1)} all-reduce(f32[80,80]{1,0:T(8,128)S(1)} %convolution_bitcast_fusion.2), channel_id=1, replica_groups=mesh['gx'=16,'gy'=8] {'gx','gy'}, use_global_device_ids=true, to_apply=%region_4.7 | all-reduce | flops 6400 | bytes 51200 | tf_op jit(solution)/shard_map/psum | solution.py:77
  525.3 5.8 cholesky.111
  532.4 4.9 custom-call.13
  547.1 4.8 collective-permute-start.54
  555.9 4.4 collective-permute-done.55
  575.9 4.4 collective-permute-done.59
  581.1 4.7 collective-permute-start.60
  626.7 66.7 %psum.38 = f32[80,80]{1,0:T(8,128)S(1)} all-reduce(f32[80,80]{1,0:T(8,128)S(1)} %convolution_bitcast_fusion.1), channel_id=1, replica_groups=mesh['gx'=16,'gy'=8] {'gx','gy'}, use_global_device_ids=true, to_apply=%region_5.8 | all-reduce | flops 6400 | bytes 51200 | tf_op jit(solution)/shard_map/psum | solution.py:77
  697.7 5.8 cholesky.122
  704.9 4.9 custom-call.14
  719.4 5.7 collective-permute-start.70
  729.1 4.4 collective-permute-done.71
  753.9 5.0 collective-permute-start.76
  776.2 4.5 collective-permute-start.80
  799.5 66.5 %psum.39 = f32[80,80]{1,0:T(8,128)S(1)} all-reduce(f32[80,80]{1,0:T(8,128)S(1)} %convolution_bitcast_fusion), channel_id=1, replica_groups=mesh['gx'=16,'gy'=8] {'gx','gy'}, use_global_device_ids=true, to_apply=%region_6.9 | all-reduce | flops 6400 | bytes 51200 | tf_op jit(solution)/shard_map/psum | solution.py:77
  867.9 5.8 cholesky.133
  875.1 4.9 custom-call.15
  (389 shorter events, 414.2 us)
Async XLA Ops:
  32.0 7.3 collective-permute-start.6
  35.3 8.4 collective-permute-start.7
  57.1 8.4 collective-permute-start.11
  78.1 8.4 collective-permute-start.15
  99.1 8.4 collective-permute-start.19
  201.0 8.9 %collective-permute-start.22 = (f32[16,4,10,1]{3,0,2,1:T(8,128)S(1)}, f32[16,4,10,1]{3,0,2,1:T(8,128)S(1)}, u32[]{:S(2)}, u32[]{:S(2)}) collective-permute-start(f32[16,4,10,1]{3,0,2,1:T(8,128)S(1)} %get-tuple-element.77), channel_id=1, source_target_pairs={{0,1},{1,2},{2,3},{3,4},{4,5},{5,6},{6,7},{8,9},{9,10},{10,11},{11... | collective-permute-start | bytes 7688 | tf_op jit(solution)/shard_map/ppermute | solution.py:19
  206.0 8.4 collective-permute-start.23
  222.8 7.3 collective-permute-start.26
  226.1 8.4 collective-permute-start.27
  245.2 7.2 collective-permute-start.30
  248.4 8.4 collective-permute-start.31
  266.2 7.2 collective-permute-start.34
  269.4 8.4 collective-permute-start.35
  374.5 8.4 collective-permute-start.38
  378.9 8.4 collective-permute-start.39
  399.0 8.4 collective-permute-start.43
  418.5 7.2 collective-permute-start.46
  421.6 8.4 collective-permute-start.47
  442.6 8.4 collective-permute-start.51
  547.1 8.8 collective-permute-start.54
  551.9 8.4 collective-permute-start.55
  571.9 8.4 collective-permute-start.59
  593.8 8.4 collective-permute-start.63
  611.9 7.4 collective-permute-start.66
  614.8 8.4 collective-permute-start.67
  719.4 9.7 %collective-permute-start.70 = (f32[16,4,10,1]{3,0,2,1:T(8,128)S(1)}, f32[16,4,10,1]{3,0,2,1:T(8,128)S(1)}, u32[]{:S(2)}, u32[]{:S(2)}) collective-permute-start(f32[16,4,10,1]{3,0,2,1:T(8,128)S(1)} %get-tuple-element.53), channel_id=1, source_target_pairs={{0,1},{1,2},{2,3},{3,4},{4,5},{5,6},{6,7},{8,9},{9,10},{10,11},{11... | collective-permute-start | bytes 7688 | tf_op jit(solution)/shard_map/ppermute | solution.py:19
  725.1 8.4 collective-permute-start.71
  741.5 7.2 collective-permute-start.74
  744.7 8.4 collective-permute-start.75
  753.9 7.6 collective-permute-start.76
  767.0 8.4 collective-permute-start.79
  788.7 8.4 collective-permute-start.83
  (64 other events, 720.1 us)
where the time goes:
time: 894 us; the launch traced here: 885 us
  blocking collectives  334 us (37%)
  starting transfers between devices  214 us (24%)
  waiting for transfers between devices  190 us (21%)
  other arithmetic  80.5 us (9%)
  matrix products  34 us (4%)
  local copies, waits for them, and re-layouts  30.1 us (3%)
    psum x5, blocking collectives, shards(): gram_all = lax.psum(local_gram, ('gx', 'gy'))  334 us
    ppermute x42, waiting for transfers between devices, padded_2(): after = lax.ppermute(leading, axis, down)  157 us
    ppermute x42, starting transfers between devices, padded_2(): before = lax.ppermute(last, axis, up)  145 us
    ppermute x42, starting transfers between devices, padded_2(): after = lax.ppermute(leading, axis, down)  68.6 us
    another operation x15, other arithmetic, small_solve(): lower = jnp.linalg.cholesky(normal)  32.6 us
    ppermute x42, waiting for transfers between devices, padded_2(): before = lax.ppermute(last, axis, up)  32.5 us
    another operation x10, other arithmetic, small_solve(): y = jax.scipy.linalg.cho_solve((lower, True), right_side)  27.7 us
    unnamed x46, local copies, waits for them, and re-layouts  18.2 us
  transfers between devices with their start and end apart: 84, of which 61 were waited for; matrix products, arithmetic and copies ran while one was open for 2% of the time, Pallas kernels for 0%

commit v1 on v0

--- a/solution.py
+++ b/solution.py
@@ -74,7 +74,12 @@
             blocks.append(-apply_off(padded, terms) / diagonal)
         stacked = jnp.concatenate(blocks, 0).reshape(BASIS, -1)
         local_gram = jnp.dot(stacked, stacked.T, precision=hp)
-        gram_all = lax.psum(local_gram, ("gx", "gy"))
+
+        def solve_the_numbers(page):
+            ready = jnp.sum(lax.all_gather(page, ("gx", "gy")), 0)
+            return ready
+
+        gram_all = solve_the_numbers(local_gram)
         y, coeffs = small_solve(gram_all)
         solution = solution + jnp.dot(y.T, stacked[: BASIS - RHS], precision=hp).reshape(shape)
         residual = jnp.dot(coeffs.T, stacked, precision=hp).reshape(shape)

time: 894 us -> 918 us (1.027)
  waiting for transfers between devices: 190 us -> 526 us
  blocking collectives: 334 us -> 0 us
  other arithmetic: 80.5 us -> 95.6 us
  between operations: 2.94 us -> 16.3 us
    psum x5 -> x0, blocking collectives: 334 us -> none  [shards(): gram_all = lax.psum(local_gram, ('gx', 'gy'))]
    all_gather x0 -> x5, waiting for transfers between devices: none -> 321 us  [solve_the_numbers(): ready = jnp.sum(lax.all_gather(page, ('gx', 'gy')), 0)]
    reduce_sum x0 -> x5, other arithmetic: none -> 14.5 us  [solve_the_numbers(): ready = jnp.sum(lax.all_gather(page, ('gx', 'gy')), 0)]
  transfers between devices with their start and end apart: 84 -> 89, of which waited for: 61 -> 67; matrix products, arithmetic and copies ran while one was open for 2% -> 3% of each run, Pallas kernels for 0% -> 0%
where the time goes in v1:
time: 918 us; the launch traced here: 910 us
  waiting for transfers between devices  526 us (57%)
  starting transfers between devices  209 us (23%)
  other arithmetic  95.6 us (10%)
  matrix products  35.4 us (4%)
  local copies, waits for them, and re-layouts  27.2 us (3%)
  between operations  16.3 us (2%)
    all_gather x5, waiting for transfers between devices, solve_the_numbers(): ready = jnp.sum(lax.all_gather(page, ('gx', 'gy')), 0)  321 us
    ppermute x42, waiting for transfers between devices, padded_2(): after = lax.ppermute(leading, axis, down)  164 us
    ppermute x42, starting transfers between devices, padded_2(): before = lax.ppermute(last, axis, up)  140 us
    ppermute x42, starting transfers between devices, padded_2(): after = lax.ppermute(leading, axis, down)  67.6 us
    ppermute x42, waiting for transfers between devices, padded_2(): before = lax.ppermute(last, axis, up)  41.3 us
    another operation x15, other arithmetic, small_solve(): lower = jnp.linalg.cholesky(normal)  32.6 us
    another operation x10, other arithmetic, small_solve(): y = jax.scipy.linalg.cho_solve((lower, True), right_side)  27.4 us
  transfers between devices with their start and end apart: 89, of which 67 were waited for; matrix products, arithmetic and copies ran while one was open for 3% of the time, Pallas kernels for 0%

profile of v1, /device:TPU:1, one launch (start us, length us, event | category | flops | bytes accessed | tf_op | source)
XLA Modules:
  0.0 910.2 jit_solution(2982100690045587182)
XLA Ops:
  17.2 5.1 collective-permute-start.2
  51.1 4.6 collective-permute-start.8
  67.7 4.4 collective-permute-done.11
  109.7 4.4 collective-permute-done.19
  119.9 67.6 %all-gather.11.cloned.1.call-done = f32[10240,80]{1,0:T(8,128)} async-done(((f32[80,80]{1,0:T(8,128)}), f32[10240,80]{1,0:T(8,128)}) %all-gather.11.cloned.1.call-update) | async-done | bytes 3276816 | tf_op jit(solution)/shard_map/all_gather | solution.py:79
  191.3 5.8 cholesky.89
  198.4 4.9 custom-call.11
  221.3 4.4 collective-permute-done.23
  246.9 4.5 collective-permute-start.28
  263.4 4.4 collective-permute-done.31
  294.2 67.0 %all-gather.13.cloned.1.call-done = f32[10240,80]{1,0:T(8,128)} async-done(((f32[80,80]{1,0:T(8,128)}), f32[10240,80]{1,0:T(8,128)}) %all-gather.13.cloned.1.call-update) | async-done | bytes 3276816 | tf_op jit(solution)/shard_map/all_gather | solution.py:79
  365.0 5.8 cholesky.100
  372.1 4.9 custom-call.12
  415.3 4.4 collective-permute-done.43
  420.5 4.5 collective-permute-start.44
  437.1 4.4 collective-permute-done.47
  458.0 4.4 collective-permute-done.51
  467.9 67.0 %all-gather.15.cloned.1.call-done = f32[10240,80]{1,0:T(8,128)} async-done(((f32[80,80]{1,0:T(8,128)}), f32[10240,80]{1,0:T(8,128)}) %all-gather.15.cloned.1.call-update) | async-done | bytes 3276816 | tf_op jit(solution)/shard_map/all_gather | solution.py:79
  538.7 5.8 cholesky.111
  545.8 4.9 custom-call.13
  594.2 4.5 collective-permute-start.60
  610.7 4.4 collective-permute-done.63
  631.7 4.4 collective-permute-done.67
  641.8 66.8 %all-gather.17.cloned.1.call-done = f32[10240,80]{1,0:T(8,128)} async-done(((f32[80,80]{1,0:T(8,128)}), f32[10240,80]{1,0:T(8,128)}) %all-gather.17.cloned.1.call-update) | async-done | bytes 3276816 | tf_op jit(solution)/shard_map/all_gather | solution.py:79
  712.4 5.8 cholesky.122
  719.5 4.9 custom-call.14
  768.3 4.5 collective-permute-start.76
  784.8 4.4 collective-permute-done.79
  805.8 4.4 collective-permute-done.83
  830.3 52.3 %all-gather.19.cloned.1.call-done = f32[10240,80]{1,0:T(8,128)} async-done(((f32[80,80]{1,0:T(8,128)}), f32[10240,80]{1,0:T(8,128)}) %all-gather.19.cloned.1.call-update) | async-done | bytes 3276816 | tf_op jit(solution)/shard_map/all_gather | solution.py:79
  886.4 5.8 cholesky.133
  893.6 4.9 custom-call.15
  (432 shorter events, 443.6 us)
Async XLA Ops:
  7.2 180.4 %all-gather.11.cloned.1.call-start = ((), (), s32[]{:S(2)}) async-start(), calls=%async_computation | async-start | bytes 5283840 | tf_op jit(solution)/shard_map/all_gather | solution.py:79
  38.5 7.3 collective-permute-start.6
  41.9 8.4 collective-permute-start.7
  63.7 8.4 collective-permute-start.11
  84.7 8.4 collective-permute-start.15
  105.7 8.4 collective-permute-start.19
  116.7 244.5 %all-gather.13.cloned.1.call-start = ((), (), s32[]{:S(2)}) async-start(), calls=%async_computation.1 | async-start | bytes 5283840 | tf_op jit(solution)/shard_map/all_gather | solution.py:79
  213.4 7.9 collective-permute-start.22
  217.3 8.4 collective-permute-start.23
  234.5 7.2 collective-permute-start.26
  237.6 8.4 collective-permute-start.27
  259.4 8.4 collective-permute-start.31
  280.4 8.4 collective-permute-start.35
  291.3 243.6 %all-gather.15.cloned.1.call-start = ((), (), s32[]{:S(2)}) async-start(), calls=%async_computation.2 | async-start | bytes 5283840 | tf_op jit(solution)/shard_map/all_gather | solution.py:79
  387.1 7.9 collective-permute-start.38
  391.0 8.4 collective-permute-start.39
  408.2 7.2 collective-permute-start.42
  411.3 8.4 collective-permute-start.43
  433.1 8.4 collective-permute-start.47
  454.0 8.4 collective-permute-start.51
  465.0 243.6 %all-gather.17.cloned.1.call-start = ((), (), s32[]{:S(2)}) async-start(), calls=%async_computation.3 | async-start | bytes 5283840 | tf_op jit(solution)/shard_map/all_gather | solution.py:79
  560.8 7.9 collective-permute-start.54
  564.7 8.4 collective-permute-start.55
  585.0 8.4 collective-permute-start.59
  606.7 8.4 collective-permute-start.63
  627.7 8.4 collective-permute-start.67
  638.7 243.9 %all-gather.19.cloned.1.call-start = ((), (), s32[]{:S(2)}) async-start(), calls=%async_computation.4 | async-start | bytes 5283840 | tf_op jit(solution)/shard_map/all_gather | solution.py:79
  734.8 7.9 collective-permute-start.70
  738.8 8.4 collective-permute-start.71
  759.1 8.4 collective-permute-start.75
  780.8 8.4 collective-permute-start.79
  801.8 8.4 collective-permute-start.83
  (83 other events, 598.3 us)
Sparse Core Ops, SparseCore 0:
  116.8 70.6 all-gather.10
  291.5 69.7 all-gather.12
  465.1 69.7 all-gather.14
  638.8 69.7 all-gather.16
  812.9 69.6 all-gather.18
